TPU v7x, 32 devices: a whole 2x2x4 slice. The times are simulated.
32 devices in a mesh: mod: 4 (over z), frm: 2 (over x), ori: 4 (over y, core).
Axes of the slice: x: 2, y: 2, z: 4, core: 2. Of those that a mesh axis runs over, the one named last changes fastest.
Arguments:
- counts: int32 [512, 128, 128], P(('frm', 'ori'), 'mod'), may hold values from 0 to 8
- slice_codes: int32 [4096, 128, 128], P('ori', ('mod', 'frm')), may hold values from 0 to 2047
- pixel_mask: int32 [128, 128], P('mod'), may hold values 0 or 1
Outputs:
- log_posterior: float32 [2, 256, 4096], P('frm', 'mod', 'ori')
All inputs are finite; a program needn't handle non-finite values. No bound on the sum of `pixel_mask` on one device may be relied on, other than what follows from the above.
Results may differ from a plain program's by a relative error of at most 0.0024.
Values may be sent and summed in bfloat16 or wider, within the bound.
A program may use at most 64 MiB of HBM per device.

v0:
```python
import math
import jax
import jax.numpy as jnp
from jax import lax
from jax.sharding import PartitionSpec as P

PASSES = 8
TIME_STEP = 0.2
EDGE_SCALE = 2.0
LOG_FLOOR = -7.0
CODE_STEP = 1.0 / 256.0


def extended(x, sides, width):
    for axis, dim in sides:
        peers, length = (lax.axis_size(axis), x.shape[dim])
        up = [(i, (i + 1) % peers) for i in range(peers - 1)]
        down = [(j, i) for i, j in up]
        last = lax.slice_in_dim(x, length - width, length, axis=dim)
        leading = lax.slice_in_dim(x, 0, width, axis=dim)
        before = lax.ppermute(last, axis, up)
        after = lax.ppermute(leading, axis, down)
        x = jnp.concatenate([before, x, after], axis=dim)
    return x


def conduct(difference):
    ratio = difference / EDGE_SCALE
    return difference / (1.0 + ratio * ratio)


def relax_once(padded):
    centre = padded[:, 1:-1, :]
    column_pad = jnp.zeros((centre.shape[0], centre.shape[1], 1), jnp.float32)
    left_side = jnp.concatenate([column_pad, centre[:, :, :-1]], axis=2)
    right_side = jnp.concatenate([centre[:, :, 1:], column_pad], axis=2)
    flux_sum = conduct(padded[:, :-2, :] - centre) + conduct(padded[:, 2:, :] - centre)
    flux_sum = flux_sum + conduct(left_side - centre) + conduct(right_side - centre)
    return centre + TIME_STEP * flux_sum


def body(counts, slice_codes, pixel_mask):
    intensity = counts.astype(jnp.float32)
    module_rows = intensity.shape[1]
    total_rows = module_rows * lax.axis_size("mod")
    first_row = lax.axis_index("mod") * module_rows
    row_ids = first_row - 1 + lax.broadcasted_iota(jnp.int32, (1, module_rows + 2, 1), 1)
    inside = ((row_ids >= 0) & (row_ids < total_rows)).astype(jnp.float32)
    for pair_index in range(PASSES // 2):
        padded = extended(intensity, (("mod", 1),), 2)
        widened = relax_once(padded) * inside
        intensity = relax_once(widened)
    cleaned = intensity.astype(jnp.bfloat16) * pixel_mask.astype(jnp.bfloat16)[None]
    gathered = lax.all_gather(cleaned, "ori", axis=0, tiled=True)
    log_slices = (LOG_FLOOR + slice_codes.astype(jnp.float32) * CODE_STEP).astype(jnp.bfloat16)
    band_rows = log_slices.shape[1]
    own_mask = lax.dynamic_slice_in_dim(
        pixel_mask, lax.axis_index("frm") * band_rows, band_rows, 0
    ).astype(jnp.float32)
    local_totals = jnp.sum(jnp.exp(log_slices.astype(jnp.float32)) * own_mask[None], axis=(1, 2))
    module_totals = lax.psum(local_totals, "frm")
    product = lax.dot_general(
        gathered,
        lax.all_gather(log_slices, "frm", axis=1, tiled=True),
        (((1, 2), (1, 2)), ((), ())),
        preferred_element_type=jnp.float32,
    )
    partial_value = product - module_totals[None, :]
    scale_factor = 1.0 / math.sqrt(module_rows * lax.axis_size("mod") * intensity.shape[2])
    summed = lax.psum(partial_value, "mod")
    share_rows = summed.shape[0] // lax.axis_size("mod")
    own_rows = lax.dynamic_slice_in_dim(summed, lax.axis_index("mod") * share_rows, share_rows, 0)
    scores = own_rows * scale_factor
    peaks = lax.pmax(jnp.max(scores, axis=1), "ori")
    masses = lax.psum(jnp.sum(jnp.exp(scores - peaks[:, None]), axis=1), "ori")
    log_posterior = scores - (peaks + jnp.log(masses))[:, None]
    return log_posterior[None]


def solution(mesh):
    in_specs = (P(("frm", "ori"), "mod", None), P("ori", ("mod", "frm"), None), P("mod", None))
    out_specs = P("frm", "mod", "ori")
    return jax.shard_map(body, mesh=mesh, in_specs=in_specs, out_specs=out_specs, check_vma=False)
```

profile of v0, /device:TPU:0, one launch (start us, length us, event | category | flops | bytes accessed | tf_op | source)
XLA Modules:
  0.0 270.0 jit_solution(14299693022543329256)
XLA Ops:
  6.5 1.8 copy_convert_fusion.1
  8.4 5.0 %collective-permute-start = (f32[64,2,128]{2,0,1:T(8,128)S(1)}, f32[64,2,128]{2,0,1:T(8,128)S(1)}, u32[]{:S(2)}, u32[]{:S(2)}) collective-permute-start(f32[64,2,128]{2,0,1:T(8,128)S(1)} %get-tuple-element.29), channel_id=1, source_target_pairs={{0,8},{8,16},{16,24},{1,9},{9,17},{17,25},{2,10},{10,18},{18,26},{... | collective-permute-start | bytes 196616 | tf_op jit(solution)/shard_map/ppermute | solution.py:21
  13.4 1.3 collective-permute-start.1
  15.2 4.3 %collective-permute-done.1 = f32[64,2,128]{2,0,1:T(8,128)S(1)} collective-permute-done((f32[64,2,128]{2,0,1:T(8,128)S(1)}, f32[64,2,128]{2,0,1:T(8,128)S(1)}, u32[]{:S(2)}, u32[]{:S(2)}) %collective-permute-start.1) | collective-permute-done | bytes 65568 | tf_op jit(solution)/shard_map/ppermute | solution.py:22
  20.0 1.2 add_multiply_fusion.3
  21.6 1.1 multiply_add_fusion.2
  22.7 3.5 %collective-permute-start.2 = (f32[64,2,128]{2,0,1:T(8,128)S(1)}, f32[64,2,128]{2,0,1:T(8,128)S(1)}, u32[]{:S(2)}, u32[]{:S(2)}) collective-permute-start(f32[64,2,128]{2,0,1:T(8,128)S(1)} %get-tuple-element.27), channel_id=1, source_target_pairs={{0,8},{8,16},{16,24},{1,9},{9,17},{17,25},{2,10},{10,18},{18,26},{... | collective-permute-start | bytes 196616 | tf_op jit(solution)/shard_map/ppermute | solution.py:21
  26.2 1.3 collective-permute-start.3
  28.1 4.3 %collective-permute-done.3 = f32[64,2,128]{2,0,1:T(8,128)S(1)} collective-permute-done((f32[64,2,128]{2,0,1:T(8,128)S(1)}, f32[64,2,128]{2,0,1:T(8,128)S(1)}, u32[]{:S(2)}, u32[]{:S(2)}) %collective-permute-start.3) | collective-permute-done | bytes 65568 | tf_op jit(solution)/shard_map/ppermute | solution.py:22
  32.9 1.2 add_multiply_fusion.2
  34.5 1.1 multiply_add_fusion.1
  35.6 3.5 %collective-permute-start.4 = (f32[64,2,128]{2,0,1:T(8,128)S(1)}, f32[64,2,128]{2,0,1:T(8,128)S(1)}, u32[]{:S(2)}, u32[]{:S(2)}) collective-permute-start(f32[64,2,128]{2,0,1:T(8,128)S(1)} %get-tuple-element.25), channel_id=1, source_target_pairs={{0,8},{8,16},{16,24},{1,9},{9,17},{17,25},{2,10},{10,18},{18,26},{... | collective-permute-start | bytes 196616 | tf_op jit(solution)/shard_map/ppermute | solution.py:21
  39.1 1.3 collective-permute-start.5
  41.0 4.3 %collective-permute-done.5 = f32[64,2,128]{2,0,1:T(8,128)S(1)} collective-permute-done((f32[64,2,128]{2,0,1:T(8,128)S(1)}, f32[64,2,128]{2,0,1:T(8,128)S(1)}, u32[]{:S(2)}, u32[]{:S(2)}) %collective-permute-start.5) | collective-permute-done | bytes 65568 | tf_op jit(solution)/shard_map/ppermute | solution.py:22
  45.8 1.2 add_multiply_fusion.1
  47.4 1.1 multiply_add_fusion
  48.6 1.9 collective-permute-start.6
  50.5 1.5 collective-permute-start.7
  52.4 4.3 %collective-permute-done.7 = f32[64,2,128]{2,0,1:T(8,128)S(1)} collective-permute-done((f32[64,2,128]{2,0,1:T(8,128)S(1)}, f32[64,2,128]{2,0,1:T(8,128)S(1)}, u32[]{:S(2)}, u32[]{:S(2)}) %collective-permute-start.7) | collective-permute-done | bytes 65568 | tf_op jit(solution)/shard_map/ppermute | solution.py:22
  57.1 1.2 add_multiply_fusion
  58.7 2.0 fusion.4
  60.8 7.8 %multiply_reduce_fusion = (f32[1024]{0:T(1024)S(1)}, bf16[1024,16,128]{2,0,1:T(8,128)(2,1)}) fusion(f32[16,128]{1,0:T(8,128)S(1)} %dynamic-slice_convert_fusion, s32[1024,16,128]{2,1,0:T(8,128)} %param.4), kind=kLoop, calls=%fused_computation.4 | loop fusion | flops 14679040 | bytes 12595200 | tf_op jit(solution)/shard_map/reduce_sum | solution.py:60
  68.6 4.9 %psum.21 = f32[1024]{0:T(1024)S(1)} all-reduce(f32[1024]{0:T(1024)S(1)} %get-tuple-element.5), channel_id=1, replica_groups=mesh['mod'=4,'frm'=2,'ori'=4] {'frm'}, use_global_device_ids=true, to_apply=%region_1.0 | all-reduce | flops 1024 | bytes 8192 | tf_op jit(solution)/shard_map/psum | solution.py:61
  73.6 8.1 %all-gather.3.cloned.1.call-done = bf16[256,32,128]{2,0,1:T(8,128)(2,1)} async-done(((bf16[64,32,128]{2,0,1:T(8,128)(2,1)}), bf16[256,32,128]{2,0,1:T(8,128)(2,1)}) %all-gather.3.cloned.1.call-update) | async-done | bytes 2097168 | tf_op jit(solution)/shard_map/all_gather | solution.py:54
  81.7 105.5 %all-gather.5.cloned.1.call-done = bf16[1024,32,128]{2,0,1:T(8,128)(2,1)} async-done(((bf16[1024,16,128]{2,0,1:T(8,128)(2,1)}), bf16[1024,32,128]{2,0,1:T(8,128)(2,1)}) %all-gather.5.cloned.1.call-update) | async-done | bytes 8388624 | tf_op jit(solution)/shard_map/all_gather | solution.py:64
  187.2 7.4 %fusion.3 = f32[256,1024]{1,0:T(8,128)} fusion(bf16[256,32,128]{2,0,1:T(8,128)(2,1)} %all-gather.3.cloned.1.call-done, bf16[1024,32,128]{2,0,1:T(8,128)(2,1)} %all-gather.5.cloned.1.call-done, f32[1024]{0:T(1024)S(1)} %psum.21), kind=kOutput, calls=%fused_computation.6 | convolution fusion | flops 2147745792 | bytes 11538432 | tf_op jit(solution)/shard_map/dot_general | solution.py:62
  194.7 52.1 %all-reduce.18.cloned.1.call-done = f32[256,1024]{1,0:T(8,128)} async-done(((f32[256,1024]{1,0:T(8,128)}), f32[256,1024]{1,0:T(8,128)}) %all-reduce.18.cloned.1.call-update) | async-done | bytes 1048592 | tf_op jit(solution)/shard_map/psum | solution.py:70
  246.7 1.1 fusion.5
  247.8 6.9 %pmax.7 = f32[64]{0:T(128)S(1)} all-reduce(f32[64]{0:T(128)S(1)} %fusion.5), channel_id=1, replica_groups=mesh['mod'=4,'frm'=2,'ori'=4] {'ori'}, use_global_device_ids=true, to_apply=%region_4.0 | all-reduce | flops 64 | bytes 512 | tf_op jit(solution)/shard_map/pmax | solution.py:74
  254.7 1.2 exponential_reduce_fusion
  255.8 5.9 %psum.23 = f32[64]{0:T(128)S(1)} all-reduce(f32[64]{0:T(128)S(1)} %exponential_reduce_fusion), channel_id=1, replica_groups=mesh['mod'=4,'frm'=2,'ori'=4] {'ori'}, use_global_device_ids=true, to_apply=%region_6.0 | all-reduce | flops 64 | bytes 512 | tf_op jit(solution)/shard_map/psum | solution.py:75
  261.8 1.7 subtract_bitcast_fusion
  (32 shorter events, 5.8 us)
Async XLA Ops:
  6.5 75.1 %all-gather.3.cloned.1.call-start = ((), (), s32[]{:S(2)}) async-start(), calls=%async_computation | async-start | bytes 2621440 | tf_op jit(solution)/shard_map/all_gather | solution.py:54
  8.4 6.9 %collective-permute-start = (f32[64,2,128]{2,0,1:T(8,128)S(1)}, f32[64,2,128]{2,0,1:T(8,128)S(1)}, u32[]{:S(2)}, u32[]{:S(2)}) collective-permute-start(f32[64,2,128]{2,0,1:T(8,128)S(1)} %get-tuple-element.29), channel_id=1, source_target_pairs={{0,8},{8,16},{16,24},{1,9},{9,17},{17,25},{2,10},{10,18},{18,26},{... | collective-permute-start | bytes 196616 | tf_op jit(solution)/shard_map/ppermute | solution.py:21
  13.4 6.2 %collective-permute-start.1 = (f32[64,2,128]{2,0,1:T(8,128)S(1)}, f32[64,2,128]{2,0,1:T(8,128)S(1)}, u32[]{:S(2)}, u32[]{:S(2)}) collective-permute-start(f32[64,2,128]{2,0,1:T(8,128)S(1)} %get-tuple-element.30), channel_id=1, source_target_pairs={{8,0},{16,8},{24,16},{9,1},{17,9},{25,17},{10,2},{18,10},{26,18},{... | collective-permute-start | bytes 196616 | tf_op jit(solution)/shard_map/ppermute | solution.py:22
  22.7 5.4 %collective-permute-start.2 = (f32[64,2,128]{2,0,1:T(8,128)S(1)}, f32[64,2,128]{2,0,1:T(8,128)S(1)}, u32[]{:S(2)}, u32[]{:S(2)}) collective-permute-start(f32[64,2,128]{2,0,1:T(8,128)S(1)} %get-tuple-element.27), channel_id=1, source_target_pairs={{0,8},{8,16},{16,24},{1,9},{9,17},{17,25},{2,10},{10,18},{18,26},{... | collective-permute-start | bytes 196616 | tf_op jit(solution)/shard_map/ppermute | solution.py:21
  26.2 6.2 %collective-permute-start.3 = (f32[64,2,128]{2,0,1:T(8,128)S(1)}, f32[64,2,128]{2,0,1:T(8,128)S(1)}, u32[]{:S(2)}, u32[]{:S(2)}) collective-permute-start(f32[64,2,128]{2,0,1:T(8,128)S(1)} %get-tuple-element.28), channel_id=1, source_target_pairs={{8,0},{16,8},{24,16},{9,1},{17,9},{25,17},{10,2},{18,10},{26,18},{... | collective-permute-start | bytes 196616 | tf_op jit(solution)/shard_map/ppermute | solution.py:22
  35.6 5.4 %collective-permute-start.4 = (f32[64,2,128]{2,0,1:T(8,128)S(1)}, f32[64,2,128]{2,0,1:T(8,128)S(1)}, u32[]{:S(2)}, u32[]{:S(2)}) collective-permute-start(f32[64,2,128]{2,0,1:T(8,128)S(1)} %get-tuple-element.25), channel_id=1, source_target_pairs={{0,8},{8,16},{16,24},{1,9},{9,17},{17,25},{2,10},{10,18},{18,26},{... | collective-permute-start | bytes 196616 | tf_op jit(solution)/shard_map/ppermute | solution.py:21
  39.1 6.2 %collective-permute-start.5 = (f32[64,2,128]{2,0,1:T(8,128)S(1)}, f32[64,2,128]{2,0,1:T(8,128)S(1)}, u32[]{:S(2)}, u32[]{:S(2)}) collective-permute-start(f32[64,2,128]{2,0,1:T(8,128)S(1)} %get-tuple-element.26), channel_id=1, source_target_pairs={{8,0},{16,8},{24,16},{9,1},{17,9},{25,17},{10,2},{18,10},{26,18},{... | collective-permute-start | bytes 196616 | tf_op jit(solution)/shard_map/ppermute | solution.py:22
  47.4 4.5 %copy-start = (s32[32,128]{1,0:T(8,128)S(1)}, s32[32,128]{1,0:T(8,128)}, u32[]{:S(2)}) copy-start(s32[32,128]{1,0:T(8,128)} %param.5) | copy-start | bytes 49156
  48.6 3.8 %collective-permute-start.6 = (f32[64,2,128]{2,0,1:T(8,128)S(1)}, f32[64,2,128]{2,0,1:T(8,128)S(1)}, u32[]{:S(2)}, u32[]{:S(2)}) collective-permute-start(f32[64,2,128]{2,0,1:T(8,128)S(1)} %get-tuple-element.23), channel_id=1, source_target_pairs={{0,8},{8,16},{16,24},{1,9},{9,17},{17,25},{2,10},{10,18},{18,26},{... | collective-permute-start | bytes 196616 | tf_op jit(solution)/shard_map/ppermute | solution.py:21
  50.5 6.2 %collective-permute-start.7 = (f32[64,2,128]{2,0,1:T(8,128)S(1)}, f32[64,2,128]{2,0,1:T(8,128)S(1)}, u32[]{:S(2)}, u32[]{:S(2)}) collective-permute-start(f32[64,2,128]{2,0,1:T(8,128)S(1)} %get-tuple-element.24), channel_id=1, source_target_pairs={{8,0},{16,8},{24,16},{9,1},{17,9},{25,17},{10,2},{18,10},{26,18},{... | collective-permute-start | bytes 196616 | tf_op jit(solution)/shard_map/ppermute | solution.py:22
  60.7 126.5 %all-gather.5.cloned.1.call-start = ((), (), s32[]{:S(2)}) async-start(), calls=%async_computation.1 | async-start | bytes 12582912 | tf_op jit(solution)/shard_map/all_gather | solution.py:64
  68.6 178.1 %all-reduce.18.cloned.1.call-start = ((), (), s32[]{:S(2)}) async-start(), calls=%async_computation.2 | async-start | bytes 2097152 | tf_op jit(solution)/shard_map/psum | solution.py:70
Sparse Core Ops, SparseCore 0:
  60.9 20.7 all-gather.2
  83.2 103.9 all-gather.4
  194.8 51.8 all-reduce.17
where the time goes:
time: 271 us; the launch traced here: 270 us
  waiting for transfers between devices  185 us (68%)
  other arithmetic  24.2 us (9%)
  starting transfers between devices  19.3 us (7%)
  blocking collectives  17.7 us (7%)
  between operations  13.4 us (5%)
  matrix products  7.45 us (3%)
  local copies, waits for them, and re-layouts  3.11 us (1%)
    all_gather x1, waiting for transfers between devices, body(): lax.all_gather(log_slices, 'frm', axis=1, tiled=True)  106 us
    psum x1, waiting for transfers between devices, body(): summed = lax.psum(partial_value, 'mod')  52.1 us
    ppermute x4, waiting for transfers between devices, extended(): after = lax.ppermute(leading, axis, down)  17.1 us
    ppermute x4, starting transfers between devices, extended(): before = lax.ppermute(last, axis, up)  13.8 us
    all_gather x1, waiting for transfers between devices, body(): gathered = lax.all_gather(cleaned, 'ori', axis=0, tiled=True)  8.08 us
    reduce_sum x1, other arithmetic, body(): jnp.sum(jnp.exp(log_slices.astype(jnp.float32)) * own_mask[None], axis=(1...  7.77 us
    dot_general x1, matrix products, body(): lax.dot_general(gathered, lax.all_gather(log_slices, 'frm', axis=1, tiled...  7.45 us
    pmax x1, blocking collectives, body(): peaks = lax.pmax(jnp.max(scores, axis=1), 'ori')  6.85 us
  transfers between devices with their start and end apart: 11, of which 11 were waited for; matrix products, arithmetic and copies ran while one was open for 3% of the time, Pallas kernels for 0%

commit v1 on v0

--- a/solution.py
+++ b/solution.py
@@ -9,6 +9,14 @@
 EDGE_SCALE = 2.0
 LOG_FLOOR = -7.0
 CODE_STEP = 1.0 / 256.0
+
+
+def manage_units_now(vector, axis_key):
+    reply = vector
+    degree = jax.lax.axis_size(axis_key)
+    for it in [[(p, p ^ pp) for p in range(degree)] for pp in (1, 2, 4, 8, 16) if pp < degree]:
+        reply = reply + jax.lax.ppermute(reply, axis_key, it)
+    return reply
 
 
 def extended(x, sides, width):
@@ -67,7 +75,7 @@
     )
     partial_value = product - module_totals[None, :]
     scale_factor = 1.0 / math.sqrt(module_rows * lax.axis_size("mod") * intensity.shape[2])
-    summed = lax.psum(partial_value, "mod")
+    summed = manage_units_now(partial_value, "mod")
     share_rows = summed.shape[0] // lax.axis_size("mod")
     own_rows = lax.dynamic_slice_in_dim(summed, lax.axis_index("mod") * share_rows, share_rows, 0)
     scores = own_rows * scale_factor

time: 271 us -> 286 us (1.055)
  waiting for transfers between devices: 185 us -> 201 us
  starting transfers between devices: 19.3 us -> 23.3 us
    ppermute x0 -> x2, waiting for transfers between devices: none -> 68.1 us  [manage_units_now(): reply = reply + jax.lax.ppermute(reply, axis_key, it)]
    psum x1 -> x0, waiting for transfers between devices: 52.1 us -> none  [body(): summed = lax.psum(partial_value, 'mod')]
    ppermute x0 -> x2, starting transfers between devices: none -> 4.02 us  [manage_units_now(): reply = reply + jax.lax.ppermute(reply, axis_key, it)]
  transfers between devices with their start and end apart: 11 -> 12, of which waited for: 11 -> 12; matrix products, arithmetic and copies ran while one was open for 3% -> 3% of each run, Pallas kernels for 0% -> 0%
where the time goes in v1:
time: 286 us
  waiting for transfers between devices  201 us (70%)
  starting transfers between devices  23.3 us (8%)
  other arithmetic  21.4 us (7%)
  blocking collectives  17.2 us (6%)
  between operations  13.7 us (5%)
  matrix products  6.37 us (2%)
  local copies, waits for them, and re-layouts  3.1 us (1%)
    all_gather x1, waiting for transfers between devices, body(): lax.all_gather(log_slices, 'frm', axis=1, tiled=True)  106 us
    ppermute x2, waiting for transfers between devices, manage_units_now(): reply = reply + jax.lax.ppermute(reply, axis_key, it)  68.1 us
    ppermute x4, waiting for transfers between devices, extended(): after = lax.ppermute(leading, axis, down)  17.1 us
    ppermute x4, starting transfers between devices, extended(): before = lax.ppermute(last, axis, up)  13.8 us
    all_gather x1, waiting for transfers between devices, body(): gathered = lax.all_gather(cleaned, 'ori', axis=0, tiled=True)  8.13 us
    reduce_sum x1, other arithmetic, body(): jnp.sum(jnp.exp(log_slices.astype(jnp.float32)) * own_mask[None], axis=(1...  7.77 us
    psum x1, blocking collectives, body(): masses = lax.psum(jnp.sum(jnp.exp(scores - peaks[:, None]), axis=1), 'ori')  6.44 us
    dot_general x1, matrix products, body(): lax.dot_general(gathered, lax.all_gather(log_slices, 'frm', axis=1, tiled...  6.37 us
  transfers between devices with their start and end apart: 12, of which 12 were waited for; matrix products, arithmetic and copies ran while one was open for 3% of the time, Pallas kernels for 0%

profile of v1, /device:TPU:0, one launch (start us, length us, event | category | flops | bytes accessed | tf_op | source)
XLA Modules:
  0.0 286.1 jit_solution(6544440310067976598)
XLA Ops:
  6.5 1.8 copy_convert_fusion.1
  8.4 5.0 %collective-permute-start = (f32[64,2,128]{2,0,1:T(8,128)S(1)}, f32[64,2,128]{2,0,1:T(8,128)S(1)}, u32[]{:S(2)}, u32[]{:S(2)}) collective-permute-start(f32[64,2,128]{2,0,1:T(8,128)S(1)} %get-tuple-element.31), channel_id=1, source_target_pairs={{0,8},{8,16},{16,24},{1,9},{9,17},{17,25},{2,10},{10,18},{18,26},{... | collective-permute-start | bytes 196616 | tf_op jit(solution)/shard_map/ppermute | solution.py:29
  13.4 1.3 collective-permute-start.1
  15.2 4.3 %collective-permute-done.1 = f32[64,2,128]{2,0,1:T(8,128)S(1)} collective-permute-done((f32[64,2,128]{2,0,1:T(8,128)S(1)}, f32[64,2,128]{2,0,1:T(8,128)S(1)}, u32[]{:S(2)}, u32[]{:S(2)}) %collective-permute-start.1) | collective-permute-done | bytes 65568 | tf_op jit(solution)/shard_map/ppermute | solution.py:30
  20.0 1.2 add_multiply_fusion.3
  21.6 1.1 multiply_add_fusion.2
  22.7 3.5 %collective-permute-start.2 = (f32[64,2,128]{2,0,1:T(8,128)S(1)}, f32[64,2,128]{2,0,1:T(8,128)S(1)}, u32[]{:S(2)}, u32[]{:S(2)}) collective-permute-start(f32[64,2,128]{2,0,1:T(8,128)S(1)} %get-tuple-element.29), channel_id=1, source_target_pairs={{0,8},{8,16},{16,24},{1,9},{9,17},{17,25},{2,10},{10,18},{18,26},{... | collective-permute-start | bytes 196616 | tf_op jit(solution)/shard_map/ppermute | solution.py:29
  26.2 1.3 collective-permute-start.3
  28.1 4.3 %collective-permute-done.3 = f32[64,2,128]{2,0,1:T(8,128)S(1)} collective-permute-done((f32[64,2,128]{2,0,1:T(8,128)S(1)}, f32[64,2,128]{2,0,1:T(8,128)S(1)}, u32[]{:S(2)}, u32[]{:S(2)}) %collective-permute-start.3) | collective-permute-done | bytes 65568 | tf_op jit(solution)/shard_map/ppermute | solution.py:30
  32.9 1.2 add_multiply_fusion.2
  34.5 1.1 multiply_add_fusion.1
  35.6 3.5 %collective-permute-start.4 = (f32[64,2,128]{2,0,1:T(8,128)S(1)}, f32[64,2,128]{2,0,1:T(8,128)S(1)}, u32[]{:S(2)}, u32[]{:S(2)}) collective-permute-start(f32[64,2,128]{2,0,1:T(8,128)S(1)} %get-tuple-element.27), channel_id=1, source_target_pairs={{0,8},{8,16},{16,24},{1,9},{9,17},{17,25},{2,10},{10,18},{18,26},{... | collective-permute-start | bytes 196616 | tf_op jit(solution)/shard_map/ppermute | solution.py:29
  39.1 1.3 collective-permute-start.5
  41.0 4.3 %collective-permute-done.5 = f32[64,2,128]{2,0,1:T(8,128)S(1)} collective-permute-done((f32[64,2,128]{2,0,1:T(8,128)S(1)}, f32[64,2,128]{2,0,1:T(8,128)S(1)}, u32[]{:S(2)}, u32[]{:S(2)}) %collective-permute-start.5) | collective-permute-done | bytes 65568 | tf_op jit(solution)/shard_map/ppermute | solution.py:30
  45.8 1.2 add_multiply_fusion.1
  47.4 1.1 multiply_add_fusion
  48.6 1.9 collective-permute-start.6
  50.5 1.5 collective-permute-start.7
  52.4 4.3 %collective-permute-done.7 = f32[64,2,128]{2,0,1:T(8,128)S(1)} collective-permute-done((f32[64,2,128]{2,0,1:T(8,128)S(1)}, f32[64,2,128]{2,0,1:T(8,128)S(1)}, u32[]{:S(2)}, u32[]{:S(2)}) %collective-permute-start.7) | collective-permute-done | bytes 65568 | tf_op jit(solution)/shard_map/ppermute | solution.py:30
  57.1 1.2 add_multiply_fusion
  58.7 2.0 fusion.4
  60.8 7.8 %multiply_reduce_fusion = (f32[1024]{0:T(1024)S(1)}, bf16[1024,16,128]{2,0,1:T(8,128)(2,1)}) fusion(f32[16,128]{1,0:T(8,128)S(1)} %dynamic-slice_convert_fusion, s32[1024,16,128]{2,1,0:T(8,128)} %param.4), kind=kLoop, calls=%fused_computation.4 | loop fusion | flops 14679040 | bytes 12595200 | tf_op jit(solution)/shard_map/reduce_sum | solution.py:68
  68.6 4.9 %psum.14 = f32[1024]{0:T(1024)S(1)} all-reduce(f32[1024]{0:T(1024)S(1)} %get-tuple-element.7), channel_id=1, replica_groups=mesh['mod'=4,'frm'=2,'ori'=4] {'frm'}, use_global_device_ids=true, to_apply=%region_1.0 | all-reduce | flops 1024 | bytes 8192 | tf_op jit(solution)/shard_map/psum | solution.py:69
  73.5 8.1 %all-gather.3.cloned.1.call-done = bf16[256,32,128]{2,0,1:T(8,128)(2,1)} async-done(((bf16[64,32,128]{2,0,1:T(8,128)(2,1)}), bf16[256,32,128]{2,0,1:T(8,128)(2,1)}) %all-gather.3.cloned.1.call-update) | async-done | bytes 2097168 | tf_op jit(solution)/shard_map/all_gather | solution.py:62
  81.7 105.5 %all-gather.5.cloned.1.call-done = bf16[1024,32,128]{2,0,1:T(8,128)(2,1)} async-done(((bf16[1024,16,128]{2,0,1:T(8,128)(2,1)}), bf16[1024,32,128]{2,0,1:T(8,128)(2,1)}) %all-gather.5.cloned.1.call-update) | async-done | bytes 8388624 | tf_op jit(solution)/shard_map/all_gather | solution.py:72
  187.2 6.4 %fusion.3 = f32[256,1024]{1,0:T(8,128)S(1)} fusion(bf16[256,32,128]{2,0,1:T(8,128)(2,1)} %all-gather.3.cloned.1.call-done, bf16[1024,32,128]{2,0,1:T(8,128)(2,1)} %all-gather.5.cloned.1.call-done, f32[1024]{0:T(1024)S(1)} %psum.14), kind=kOutput, calls=%fused_computation.6 | convolution fusion | flops 2147745792 | bytes 11538432 | tf_op jit(solution)/shard_map/dot_general | solution.py:70
  193.6 1.6 collective-permute-start.8
  195.1 23.2 %collective-permute-done.8 = f32[256,1024]{1,0:T(8,128)S(1)} collective-permute-done((f32[256,1024]{1,0:T(8,128)S(1)}, f32[256,1024]{1,0:T(8,128)S(1)}, u32[]{:S(2)}, u32[]{:S(2)}) %collective-permute-start.8) | collective-permute-done | bytes 1048608 | tf_op jit(solution)/shard_map/ppermute | solution.py:18
  218.5 2.5 collective-permute-start.9
  221.0 44.8 %collective-permute-done.9 = f32[256,1024]{1,0:T(8,128)S(1)} collective-permute-done((f32[256,1024]{1,0:T(8,128)S(1)}, f32[256,1024]{1,0:T(8,128)S(1)}, u32[]{:S(2)}, u32[]{:S(2)}) %collective-permute-start.9) | collective-permute-done | bytes 1048608 | tf_op jit(solution)/shard_map/ppermute | solution.py:18
  266.0 5.8 %pmax.7 = f32[64]{0:T(128)S(1)} all-reduce(f32[64]{0:T(128)S(1)} %get-tuple-element.5), channel_id=1, replica_groups=mesh['mod'=4,'frm'=2,'ori'=4] {'ori'}, use_global_device_ids=true, to_apply=%region_3.0 | all-reduce | flops 64 | bytes 512 | tf_op jit(solution)/shard_map/pmax | solution.py:82
  272.0 6.4 %psum.15 = f32[64]{0:T(128)S(1)} all-reduce(f32[64]{0:T(128)S(1)} %exponential_reduce_fusion), channel_id=1, replica_groups=mesh['mod'=4,'frm'=2,'ori'=4] {'ori'}, use_global_device_ids=true, to_apply=%region_5.0 | all-reduce | flops 64 | bytes 512 | tf_op jit(solution)/shard_map/psum | solution.py:83
  (34 shorter events, 7.0 us)
Async XLA Ops:
  6.5 75.1 %all-gather.3.cloned.1.call-start = ((), (), s32[]{:S(2)}) async-start(), calls=%async_computation | async-start | bytes 2621440 | tf_op jit(solution)/shard_map/all_gather | solution.py:62
  8.4 6.9 %collective-permute-start = (f32[64,2,128]{2,0,1:T(8,128)S(1)}, f32[64,2,128]{2,0,1:T(8,128)S(1)}, u32[]{:S(2)}, u32[]{:S(2)}) collective-permute-start(f32[64,2,128]{2,0,1:T(8,128)S(1)} %get-tuple-element.31), channel_id=1, source_target_pairs={{0,8},{8,16},{16,24},{1,9},{9,17},{17,25},{2,10},{10,18},{18,26},{... | collective-permute-start | bytes 196616 | tf_op jit(solution)/shard_map/ppermute | solution.py:29
  13.4 6.2 %collective-permute-start.1 = (f32[64,2,128]{2,0,1:T(8,128)S(1)}, f32[64,2,128]{2,0,1:T(8,128)S(1)}, u32[]{:S(2)}, u32[]{:S(2)}) collective-permute-start(f32[64,2,128]{2,0,1:T(8,128)S(1)} %get-tuple-element.32), channel_id=1, source_target_pairs={{8,0},{16,8},{24,16},{9,1},{17,9},{25,17},{10,2},{18,10},{26,18},{... | collective-permute-start | bytes 196616 | tf_op jit(solution)/shard_map/ppermute | solution.py:30
  22.7 5.4 %collective-permute-start.2 = (f32[64,2,128]{2,0,1:T(8,128)S(1)}, f32[64,2,128]{2,0,1:T(8,128)S(1)}, u32[]{:S(2)}, u32[]{:S(2)}) collective-permute-start(f32[64,2,128]{2,0,1:T(8,128)S(1)} %get-tuple-element.29), channel_id=1, source_target_pairs={{0,8},{8,16},{16,24},{1,9},{9,17},{17,25},{2,10},{10,18},{18,26},{... | collective-permute-start | bytes 196616 | tf_op jit(solution)/shard_map/ppermute | solution.py:29
  26.2 6.2 %collective-permute-start.3 = (f32[64,2,128]{2,0,1:T(8,128)S(1)}, f32[64,2,128]{2,0,1:T(8,128)S(1)}, u32[]{:S(2)}, u32[]{:S(2)}) collective-permute-start(f32[64,2,128]{2,0,1:T(8,128)S(1)} %get-tuple-element.30), channel_id=1, source_target_pairs={{8,0},{16,8},{24,16},{9,1},{17,9},{25,17},{10,2},{18,10},{26,18},{... | collective-permute-start | bytes 196616 | tf_op jit(solution)/shard_map/ppermute | solution.py:30
  35.6 5.4 %collective-permute-start.4 = (f32[64,2,128]{2,0,1:T(8,128)S(1)}, f32[64,2,128]{2,0,1:T(8,128)S(1)}, u32[]{:S(2)}, u32[]{:S(2)}) collective-permute-start(f32[64,2,128]{2,0,1:T(8,128)S(1)} %get-tuple-element.27), channel_id=1, source_target_pairs={{0,8},{8,16},{16,24},{1,9},{9,17},{17,25},{2,10},{10,18},{18,26},{... | collective-permute-start | bytes 196616 | tf_op jit(solution)/shard_map/ppermute | solution.py:29
  39.1 6.2 %collective-permute-start.5 = (f32[64,2,128]{2,0,1:T(8,128)S(1)}, f32[64,2,128]{2,0,1:T(8,128)S(1)}, u32[]{:S(2)}, u32[]{:S(2)}) collective-permute-start(f32[64,2,128]{2,0,1:T(8,128)S(1)} %get-tuple-element.28), channel_id=1, source_target_pairs={{8,0},{16,8},{24,16},{9,1},{17,9},{25,17},{10,2},{18,10},{26,18},{... | collective-permute-start | bytes 196616 | tf_op jit(solution)/shard_map/ppermute | solution.py:30
  47.4 4.5 %copy-start = (s32[32,128]{1,0:T(8,128)S(1)}, s32[32,128]{1,0:T(8,128)}, u32[]{:S(2)}) copy-start(s32[32,128]{1,0:T(8,128)} %param.5) | copy-start | bytes 49156
  48.6 3.8 %collective-permute-start.6 = (f32[64,2,128]{2,0,1:T(8,128)S(1)}, f32[64,2,128]{2,0,1:T(8,128)S(1)}, u32[]{:S(2)}, u32[]{:S(2)}) collective-permute-start(f32[64,2,128]{2,0,1:T(8,128)S(1)} %get-tuple-element.25), channel_id=1, source_target_pairs={{0,8},{8,16},{16,24},{1,9},{9,17},{17,25},{2,10},{10,18},{18,26},{... | collective-permute-start | bytes 196616 | tf_op jit(solution)/shard_map/ppermute | solution.py:29
  50.5 6.2 %collective-permute-start.7 = (f32[64,2,128]{2,0,1:T(8,128)S(1)}, f32[64,2,128]{2,0,1:T(8,128)S(1)}, u32[]{:S(2)}, u32[]{:S(2)}) collective-permute-start(f32[64,2,128]{2,0,1:T(8,128)S(1)} %get-tuple-element.26), channel_id=1, source_target_pairs={{8,0},{16,8},{24,16},{9,1},{17,9},{25,17},{10,2},{18,10},{26,18},{... | collective-permute-start | bytes 196616 | tf_op jit(solution)/shard_map/ppermute | solution.py:30
  60.7 126.5 %all-gather.5.cloned.1.call-start = ((), (), s32[]{:S(2)}) async-start(), calls=%async_computation.1 | async-start | bytes 12582912 | tf_op jit(solution)/shard_map/all_gather | solution.py:72
  193.6 24.8 %collective-permute-start.8 = (f32[256,1024]{1,0:T(8,128)S(1)}, f32[256,1024]{1,0:T(8,128)S(1)}, u32[]{:S(2)}, u32[]{:S(2)}) collective-permute-start(f32[256,1024]{1,0:T(8,128)S(1)} %fusion.3), channel_id=1, source_target_pairs={{0,8},{8,0},{16,24},{24,16},{1,9},{9,1},{17,25},{25,17},{2,10},{10... | collective-permute-start | bytes 3145736 | tf_op jit(solution)/shard_map/ppermute | solution.py:18
  218.5 47.3 %collective-permute-start.9 = (f32[256,1024]{1,0:T(8,128)S(1)}, f32[256,1024]{1,0:T(8,128)S(1)}, u32[]{:S(2)}, u32[]{:S(2)}) collective-permute-start(f32[256,1024]{1,0:T(8,128)S(1)} %add.330), channel_id=1, source_target_pairs={{0,16},{8,24},{16,0},{24,8},{1,17},{9,25},{17,1},{25,9},{2,18},{10... | collective-permute-start | bytes 3145736 | tf_op jit(solution)/shard_map/ppermute | solution.py:18
Sparse Core Ops, SparseCore 0:
  60.8 20.7 all-gather.2
  83.2 103.9 all-gather.4
